TPU v7x, 32 devices: a whole 2x2x4 slice. The times are simulated.
32 devices in a mesh: dp: 2 (over core), expert: 4 (over y, x), tensor: 4 (over z).
Axes of the slice: x: 2, y: 2, z: 4, core: 2. Of those that a mesh axis runs over, the one named last changes fastest.
Arguments:
- grad_out: bfloat16 [1024, 3584], P(('dp', 'expert')), may hold values from -6 to 6
- layer_in: bfloat16 [1024, 3584], P(('dp', 'expert')), may hold values from -6 to 6
- routes: int32 [1024, 8], P(('dp', 'expert')), may hold values from 0 to 255, as said below
- combine: float32 [1024, 8], P(('dp', 'expert')), may hold values from 0.2 to 1
- gate_weight: bfloat16 [4, 3584, 1024], P('expert', 'dp', 'tensor'), may hold values from -0.09375 to 0.09375
- up_weight: bfloat16 [4, 3584, 1024], P('expert', 'dp', 'tensor'), may hold values from -0.09375 to 0.09375
- down_weight: bfloat16 [4, 1024, 3584], P('expert', 'tensor', 'dp'), may hold values from -0.1875 to 0.1875
Outputs:
- grad_in: bfloat16 [1024, 3584], P(('dp', 'expert'))
- grad_gate: bfloat16 [4, 3584, 1024], P('expert', 'dp', 'tensor')
- grad_up: bfloat16 [4, 3584, 1024], P('expert', 'dp', 'tensor')
- grad_down: bfloat16 [4, 1024, 3584], P('expert', 'tensor', 'dp')
Inputs may be any that keep to these rules, and one draw needn't show every extreme that they name: `routes`: each row names 8 different experts. In every block of 128 tokens (the tokens of one device) each expert below 4 is named by 1 to 8 tokens, and one such expert, the same for all blocks of a draw, is named by exactly 8 tokens of every block.
All inputs are finite; a program needn't handle non-finite values.
Results may differ from a plain program's by a relative error of at most 0.011.
Values may be sent and summed in bfloat16 or wider, within the bound.
A program may use at most 128 MiB of HBM per device.

v0:
```python
import jax
import jax.numpy as jnp
from jax import lax
from jax.sharding import PartitionSpec as P

CAP = 8


def expert_backward(in_rows, grad_rows, gate_w, up_w, down_w):
    gate = jnp.dot(in_rows, gate_w, preferred_element_type=jnp.float32)
    up = jnp.dot(in_rows, up_w, preferred_element_type=jnp.float32)
    sigma = jax.nn.sigmoid(gate)
    silu_gate = gate * sigma
    act = (silu_gate * up).astype(jnp.bfloat16)
    dhid = lax.dot_general(
        grad_rows, down_w, (((1,), (1,)), ((), ())), preferred_element_type=jnp.float32
    )
    d_up = (dhid * silu_gate).astype(jnp.bfloat16)
    d_gate = (dhid * up * sigma * (1.0 + gate * (1.0 - sigma))).astype(jnp.bfloat16)
    return (act, d_gate, d_up)


def slot_rows(owner, factor, layer_in, grad_out):
    tokens = layer_in.shape[0]
    lead = owner.shape
    flat_owner = owner.reshape(-1)
    picker = (flat_owner[:, None] == jnp.arange(tokens, dtype=jnp.int32)[None, :]).astype(
        jnp.bfloat16
    )
    in_rows = jnp.dot(picker, layer_in, preferred_element_type=jnp.float32).astype(jnp.bfloat16)
    grad_pick = jnp.dot(picker, grad_out, preferred_element_type=jnp.float32)
    grad_rows = (grad_pick * factor.reshape(-1)[:, None]).astype(jnp.bfloat16)
    width = layer_in.shape[1]
    return (in_rows.reshape(lead + (width,)), grad_rows.reshape(lead + (width,)))


def select_sum(positions, rows):
    count = rows.shape[0]
    labels = jnp.arange(count, dtype=jnp.int32)
    selector = jnp.sum(
        (positions[:, :, None] == labels[None, None, :]).astype(jnp.int32), axis=1
    ).astype(jnp.bfloat16)
    return jnp.dot(selector, rows, preferred_element_type=jnp.float32)


def body(grad_out, layer_in, routes, combine, gate_weight, up_weight, down_weight):
    experts = lax.axis_size("expert")
    tokens, width = grad_out.shape
    labels = jnp.arange(experts, dtype=jnp.int32)
    hits = routes[:, :, None] == labels[None, None, :]
    chosen = jnp.sum(hits, axis=1, dtype=jnp.int32)
    before = jnp.cumsum(chosen, axis=0) - chosen
    slot_of = labels[None, :] * CAP + before
    dump_row = experts * CAP
    target = jnp.where(chosen > 0, slot_of, dump_row)
    token_ids = jnp.broadcast_to(jnp.arange(tokens, dtype=jnp.int32)[:, None] + 1, target.shape)
    owner = (
        jnp.zeros((dump_row + 1,), jnp.int32)
        .at[target.reshape(-1)]
        .set(token_ids.reshape(-1))[:dump_row]
        - 1
    )
    scale_of = jnp.sum(jnp.where(hits, combine[:, :, None], jnp.zeros((), jnp.float32)), axis=1)
    factor = (
        jnp.zeros((dump_row + 1,), jnp.float32)
        .at[target.reshape(-1)]
        .set(scale_of.reshape(-1))[:dump_row]
    )
    owner = owner.reshape(experts, CAP)
    factor = factor.reshape(experts, CAP)
    pair_pos = jnp.sum(jnp.where(hits, slot_of[:, None, :], 0), axis=2) + dump_row * (
        1 - jnp.sum(hits, axis=2, dtype=jnp.int32)
    )
    in_rows, grad_rows = slot_rows(owner, factor, layer_in, grad_out)
    in_rows, grad_rows = (
        lax.all_to_all(in_rows, "expert", split_axis=0, concat_axis=0, tiled=True),
        lax.all_to_all(grad_rows, "expert", split_axis=0, concat_axis=0, tiled=True),
    )
    gate_full, up_full = (
        lax.all_gather(gate_weight[0], "dp", axis=0, tiled=True),
        lax.all_gather(up_weight[0], "dp", axis=0, tiled=True),
    )
    down_full = lax.all_gather(down_weight[0], "dp", axis=1, tiled=True)
    flat_in = in_rows.reshape(experts * CAP, width)
    flat_grad = grad_rows.reshape(experts * CAP, width)
    act, d_gate, d_up = expert_backward(flat_in, flat_grad, gate_full, up_full, down_full)
    row_grad = lax.dot_general(
        d_gate, gate_full, (((1,), (1,)), ((), ())), preferred_element_type=jnp.float32
    )
    row_grad = row_grad + lax.dot_general(
        d_up, up_full, (((1,), (1,)), ((), ())), preferred_element_type=jnp.float32
    )
    row_part = lax.psum_scatter(
        row_grad.reshape(experts, CAP, width).astype(jnp.bfloat16),
        "tensor",
        scatter_dimension=1,
        tiled=True,
    )
    returned = lax.all_to_all(row_part, "expert", split_axis=0, concat_axis=0, tiled=True)
    quarter_in = flat_in * jnp.asarray(0.25, jnp.bfloat16)
    quarter_act = act * jnp.asarray(0.25, jnp.bfloat16)
    term_gate = lax.dot_general(
        quarter_in, d_gate, (((0,), (0,)), ((), ())), preferred_element_type=jnp.float32
    )
    term_up = lax.dot_general(
        quarter_in, d_up, (((0,), (0,)), ((), ())), preferred_element_type=jnp.float32
    )
    term_down = lax.dot_general(
        quarter_act, flat_grad, (((0,), (0,)), ((), ())), preferred_element_type=jnp.float32
    )
    grad_gate, grad_up = (
        lax.psum_scatter(
            term_gate.astype(jnp.bfloat16), "dp", scatter_dimension=0, tiled=True
        ).astype(jnp.float32),
        lax.psum_scatter(
            term_up.astype(jnp.bfloat16), "dp", scatter_dimension=0, tiled=True
        ).astype(jnp.float32),
    )
    grad_down = lax.psum_scatter(
        term_down.astype(jnp.bfloat16), "dp", scatter_dimension=1, tiled=True
    )
    whole_rows = lax.all_gather(returned, "tensor", axis=1, tiled=True)
    total = select_sum(pair_pos, whole_rows.reshape(experts * CAP, width))
    return (
        total.astype(jnp.bfloat16),
        grad_gate.astype(jnp.bfloat16)[None],
        grad_up.astype(jnp.bfloat16)[None],
        grad_down[None],
    )


def solution(mesh):
    return jax.shard_map(
        body,
        mesh=mesh,
        in_specs=(
            P(("dp", "expert"), None),
            P(("dp", "expert"), None),
            P(("dp", "expert"), None),
            P(("dp", "expert"), None),
            P("expert", "dp", "tensor"),
            P("expert", "dp", "tensor"),
            P("expert", "tensor", "dp"),
        ),
        out_specs=(
            P(("dp", "expert"), None),
            P("expert", "dp", "tensor"),
            P("expert", "dp", "tensor"),
            P("expert", "tensor", "dp"),
        ),
        check_vma=False,
    )
```

profile of v0, /device:TPU:0, one launch (start us, length us, event | category | flops | bytes accessed | tf_op | source)
XLA Modules:
  0.0 136.2 jit_solution(9007823839613026142)
XLA Ops:
  7.2 0.0 copy-start
  7.2 0.0 copy-start.3
  7.2 0.0 all-gather.9.cloned.1.call-start
  7.2 0.7 all-gather.9.cloned.1.call-update
  7.9 0.0 copy-start.4
  7.9 0.0 all-gather.11.cloned.1.call-start
  8.0 0.7 all-gather.11.cloned.1.call-update
  8.7 0.0 copy-start.2
  8.7 0.0 all-gather.7.cloned.1.call-start
  8.7 0.7 all-gather.7.cloned.1.call-update
  9.4 0.0 copy-done.3
  9.5 0.1 copy.38
  9.6 0.2 reduce_window_sum.11
  9.7 0.1 copy.39
  9.8 0.1 compare_select_fusion.1
  9.9 0.1 copy.40
  10.0 0.1 select_n.36
  10.1 0.1 broadcast_in_dim.63
  10.2 0.1 reshape.139
  10.3 2.4 %scatter_custom_fusion = s32[33]{0:T(128)S(1)} fusion(s32[512]{0:T(512)S(1)} %bitcast.51, s32[512]{0:T(512)S(1)} %reshape.139, s32[]{:T(128)} %constant.10.clone.1), kind=kCustom, calls=%fused_computation.60 | custom fusion | bytes 136 | tf_op jit(solution)/shard_map/scatter | solution.py:60
  12.8 0.0 copy-done
  12.8 1.0 fusion.2
  13.8 5.2 %all-to-all-start.1 = ((bf16[4,8,3584]{2,1,0:T(8,128)(2,1)}), bf16[4,8,3584]{2,1,0:T(8,128)(2,1)S(1)}, u32[]{:S(2)}, u32[]{:S(2)}) async-start(bf16[4,8,3584]{2,1,0:T(8,128)(2,1)} %fusion.2), calls=%async_computation.1 | async-start | bytes 458752 | tf_op jit(solution)/shard_map/all_to_all | solution.py:76
  19.0 0.0 copy-done.4
  19.0 0.1 copy.41
  19.1 0.1 reshape.147
  19.2 2.4 %scatter_custom_fusion.1 = f32[33]{0:T(128)S(1)} fusion(s32[512]{0:T(512)S(1)} %bitcast.52, f32[512]{0:T(512)S(1)} %reshape.147, f32[]{:T(128)} %constant.15.clone.1), kind=kCustom, calls=%fused_computation.58 | custom fusion | bytes 136 | tf_op jit(solution)/shard_map/scatter | solution.py:67
  21.7 0.0 copy-done.2
  21.7 1.0 fusion.3
  22.7 1.6 %all-to-all-done.1 = bf16[4,8,3584]{2,1,0:T(8,128)(2,1)S(1)} async-done(((bf16[4,8,3584]{2,1,0:T(8,128)(2,1)}), bf16[4,8,3584]{2,1,0:T(8,128)(2,1)S(1)}, u32[]{:S(2)}, u32[]{:S(2)}) %all-to-all-start.1) | async-done | bytes 229408 | tf_op jit(solution)/shard_map/all_to_all | solution.py:76
  24.3 3.4 %all-to-all-start = ((bf16[4,8,3584]{2,1,0:T(8,128)(2,1)}), bf16[4,8,3584]{2,1,0:T(8,128)(2,1)S(1)}, u32[]{:S(2)}, u32[]{:S(2)}) async-start(bf16[4,8,3584]{2,1,0:T(8,128)(2,1)} %fusion.3), calls=%async_computation | async-start | bytes 458752 | tf_op jit(solution)/shard_map/all_to_all | solution.py:77
  27.7 0.0 all-reduce.3.cloned.1.call-start
  27.7 0.0 all-gather.9.cloned.1.call-done
  27.8 1.9 %fusion.10 = f32[32,256]{1,0:T(8,128)S(1)} fusion(bf16[1,3584,256]{2,1,0:T(8,128)(2,1)} %all-gather.9.cloned.1.call-done, bf16[4,8,3584]{2,1,0:T(8,128)(2,1)S(1)} %all-to-all-done.1), kind=kOutput, calls=%fused_computation.19 | convolution fusion | flops 58720256 | bytes 2097152 | tf_op jit(solution)/shard_map/dot_general | solution.py:11
  29.7 5.8 %all-gather.11.cloned.1.call-done = bf16[1,3584,256]{2,1,0:T(8,128)(2,1)} async-done(((bf16[1,1792,256]{2,1,0:T(8,128)(2,1)}), bf16[1,3584,256]{2,1,0:T(8,128)(2,1)}) %all-gather.11.cloned.1.call-update) | async-done | bytes 1835024 | tf_op jit(solution)/shard_map/all_gather | solution.py:80
  35.5 1.9 %fusion.7 = f32[32,256]{1,0:T(8,128)S(1)} fusion(bf16[1,3584,256]{2,1,0:T(8,128)(2,1)} %all-gather.11.cloned.1.call-done, bf16[4,8,3584]{2,1,0:T(8,128)(2,1)S(1)} %all-to-all-done.1), kind=kOutput, calls=%fused_computation.16 | convolution fusion | flops 58720256 | bytes 2097152 | tf_op jit(solution)/shard_map/dot_general | solution.py:10
  37.4 0.0 copy-start.1
  37.4 0.0 all-to-all-done
  37.4 11.0 %all-gather.7.cloned.1.call-done = bf16[1,256,3584]{2,1,0:T(8,128)(2,1)} async-done(((bf16[1,256,1792]{2,1,0:T(8,128)(2,1)}), bf16[1,256,3584]{2,1,0:T(8,128)(2,1)}) %all-gather.7.cloned.1.call-update) | async-done | bytes 1835024 | tf_op jit(solution)/shard_map/all_gather | solution.py:83
  48.4 2.1 %multiply_convert_fusion.1 = (bf16[32,256]{1,0:T(8,128)(2,1)S(1)}, bf16[32,256]{1,0:T(8,128)(2,1)S(1)}) fusion(f32[32,256]{1,0:T(8,128)S(1)} %fusion.7, f32[32,256]{1,0:T(8,128)S(1)} %fusion.10, bf16[1,256,3584]{2,1,0:T(8,128)(2,1)} %all-gather.7.cloned.1.call-done, bf16[4,8,3584]{2,1,0:T(8,128)(2,1)S(1)} %all-to-all-done), kind=kOutput, calls=%fused_computation.35 | convolution fusion | flops 58826752 | bytes 2162688 | tf_op jit(solution)/shard_map/dot_general | solution.py:15
  50.5 2.1 %fusion.5 = f32[32,3584]{1,0:T(8,128)S(1)} fusion(bf16[32,256]{1,0:T(8,128)(2,1)S(1)} %get-tuple-element.9, bf16[1,3584,256]{2,1,0:T(8,128)(2,1)} %all-gather.11.cloned.1.call-done), kind=kOutput, calls=%fused_computation.14 | convolution fusion | flops 58720256 | bytes 2310144 | tf_op jit(solution)/shard_map/dot_general | solution.py:87
  52.7 0.6 fusion.4
  53.3 0.8 copy.42
  54.2 0.0 all-reduce.3.cloned.1.call-update
  54.2 0.0 reduce-scatter.4.cloned.1.call-start
  54.2 1.9 %convolution_convert_fusion.2 = bf16[3584,256]{1,0:T(8,128)(2,1)} fusion(bf16[32,256]{1,0:T(8,128)(2,1)S(1)} %get-tuple-element.9, bf16[4,8,3584]{2,1,0:T(8,128)(2,1)S(1)} %all-to-all-done.1), kind=kOutput, calls=%fused_computation.4 | convolution fusion | flops 59752448 | bytes 2080768 | tf_op jit(solution)/shard_map/dot_general | solution.py:102
  56.2 0.0 reduce-scatter.4.cloned.1.call-update
  56.2 0.0 reduce-scatter.6.cloned.1.call-start
  56.2 1.9 %convolution_convert_fusion.1 = bf16[3584,256]{1,0:T(8,128)(2,1)} fusion(bf16[32,256]{1,0:T(8,128)(2,1)S(1)} %get-tuple-element.8, bf16[4,8,3584]{2,1,0:T(8,128)(2,1)S(1)} %all-to-all-done.1), kind=kOutput, calls=%fused_computation.3 | convolution fusion | flops 59752448 | bytes 2080768 | tf_op jit(solution)/shard_map/dot_general | solution.py:105
  58.2 0.0 reduce-scatter.6.cloned.1.call-update
  58.2 0.0 copy-start.5
  58.2 0.0 reduce-scatter.8.cloned.1.call-start
  58.2 1.9 %convolution_convert_fusion = bf16[256,3584]{1,0:T(8,128)(2,1)} fusion(bf16[4,8,3584]{2,1,0:T(8,128)(2,1)S(1)} %all-to-all-done, f32[32,256]{1,0:T(8,128)S(1)} %fusion.10, f32[32,256]{1,0:T(8,128)S(1)} %fusion.7), kind=kOutput, calls=%fused_computation.2 | convolution fusion | flops 59695104 | bytes 2129920 | tf_op jit(solution)/shard_map/dot_general | solution.py:108
  60.2 0.0 reduce-scatter.8.cloned.1.call-update
  60.2 0.6 dynamic-slice
  61.4 29.3 %all-reduce.3.cloned.1.call-done = bf16[4,8,3584]{2,0,1:T(4,128)(2,1)} async-done(((bf16[4,8,3584]{2,0,1:T(4,128)(2,1)}), bf16[4,8,3584]{2,0,1:T(4,128)(2,1)}) %all-reduce.3.cloned.1.call-update) | async-done | bytes 229392
  90.7 0.8 constant_dynamic-slice_fusion
  91.6 0.7 copy.43
  92.3 3.6 %all-to-all-start.2 = ((bf16[4,2,3584]{2,1,0:T(2,128)(2,1)}), bf16[4,2,3584]{2,1,0:T(2,128)(2,1)S(1)}, u32[]{:S(2)}, u32[]{:S(2)}) async-start(bf16[4,2,3584]{2,1,0:T(2,128)(2,1)} %copy.43), calls=%async_computation.2 | async-start | bytes 114688 | tf_op jit(solution)/shard_map/all_to_all | solution.py:99
  95.9 4.8 %all-to-all-done.2 = bf16[4,2,3584]{2,1,0:T(2,128)(2,1)S(1)} async-done(((bf16[4,2,3584]{2,1,0:T(2,128)(2,1)}), bf16[4,2,3584]{2,1,0:T(2,128)(2,1)S(1)}, u32[]{:S(2)}, u32[]{:S(2)}) %all-to-all-start.2) | async-done | bytes 57376 | tf_op jit(solution)/shard_map/all_to_all | solution.py:99
  100.7 13.7 %all_gather.15 = bf16[4,8,3584]{2,0,1:T(4,128)(2,1)S(1)} all-gather(bf16[4,2,3584]{2,0,1:T(4,128)(2,1)S(1)} %copy.44), channel_id=1, replica_groups=mesh['dp'=2,'expert'=4,'tensor'=4] {'tensor'}, dimensions={1}, use_global_device_ids=true | all-gather | bytes 286720 | tf_op jit(solution)/shard_map/all_gather | solution.py:122
  114.4 1.3 convolution_convert_fusion.3
  115.8 0.2 reduce-scatter.6.cloned.1.call-done
  116.0 13.4 %reduce-scatter.8.cloned.1.call-done = bf16[256,1792]{1,0:T(8,128)(2,1)} async-done(((bf16[256,3584]{1,0:T(8,128)(2,1)}), bf16[256,1792]{1,0:T(8,128)(2,1)}) %reduce-scatter.8.cloned.1.call-update) | async-done | bytes 917520 | tf_op jit(solution)/shard_map/reduce_scatter | solution.py:119
  (13 shorter events, 0.1 us)
Async XLA Ops:
  7.2 5.6 %copy-start = (bf16[128,3584]{1,0:T(8,128)(2,1)S(1)}, bf16[128,3584]{1,0:T(8,128)(2,1)}, u32[]{:S(2)}) copy-start(bf16[128,3584]{1,0:T(8,128)(2,1)} %param.8) | copy-start | bytes 2752516
  7.2 2.3 %copy-start.3 = (s32[128,8]{0,1:T(8,128)S(1)}, s32[128,8]{0,1:T(8,128)}, u32[]{:S(2)}) copy-start(s32[128,8]{0,1:T(8,128)} %param.9) | copy-start | bytes 12292
  7.2 20.6 %all-gather.9.cloned.1.call-start = ((), (), s32[]{:S(2)}) async-start(), calls=%async_computation.10 | async-start | bytes 2752512 | tf_op jit(solution)/shard_map/all_gather | solution.py:81
  7.9 11.1 %copy-start.4 = (f32[128,8]{0,1:T(8,128)S(1)}, f32[128,8]{0,1:T(8,128)}, u32[]{:S(2)}) copy-start(f32[128,8]{0,1:T(8,128)} %param.10) | copy-start | bytes 12292
  7.9 27.5 %all-gather.11.cloned.1.call-start = ((), (), s32[]{:S(2)}) async-start(), calls=%async_computation.11 | async-start | bytes 2752512 | tf_op jit(solution)/shard_map/all_gather | solution.py:80
  8.7 13.0 %copy-start.2 = (bf16[128,3584]{1,0:T(8,128)(2,1)S(1)}, bf16[128,3584]{1,0:T(8,128)(2,1)}, u32[]{:S(2)}) copy-start(bf16[128,3584]{1,0:T(8,128)(2,1)} %param.7) | copy-start | bytes 2752516
  8.7 39.7 %all-gather.7.cloned.1.call-start = ((), (), s32[]{:S(2)}) async-start(), calls=%async_computation.9 | async-start | bytes 2752512 | tf_op jit(solution)/shard_map/all_gather | solution.py:83
  13.8 10.5 %all-to-all-start.1 = ((bf16[4,8,3584]{2,1,0:T(8,128)(2,1)}), bf16[4,8,3584]{2,1,0:T(8,128)(2,1)S(1)}, u32[]{:S(2)}, u32[]{:S(2)}) async-start(bf16[4,8,3584]{2,1,0:T(8,128)(2,1)} %fusion.2), calls=%async_computation.1 | async-start | bytes 458752 | tf_op jit(solution)/shard_map/all_to_all | solution.py:76
  24.3 13.1 %all-to-all-start = ((bf16[4,8,3584]{2,1,0:T(8,128)(2,1)}), bf16[4,8,3584]{2,1,0:T(8,128)(2,1)S(1)}, u32[]{:S(2)}, u32[]{:S(2)}) async-start(bf16[4,8,3584]{2,1,0:T(8,128)(2,1)} %fusion.3), calls=%async_computation | async-start | bytes 458752 | tf_op jit(solution)/shard_map/all_to_all | solution.py:77
  27.7 63.1 %all-reduce.3.cloned.1.call-start = ((), (), s32[]{:S(2)}) async-start(), calls=%async_computation.12 | async-start | bytes 458752
  37.4 15.3 %copy-start.1 = (bf16[1,3584,256]{2,1,0:T(8,128)(2,1)S(1)}, bf16[1,3584,256]{2,1,0:T(8,128)(2,1)}, u32[]{:S(2)}) copy-start(bf16[1,3584,256]{2,1,0:T(8,128)(2,1)} %all-gather.9.cloned.1.call-done) | copy-start | bytes 5505028
  54.2 61.6 %reduce-scatter.4.cloned.1.call-start = ((), (), s32[]{:S(2)}) async-start(), calls=%async_computation.6 | async-start | bytes 2752512 | tf_op jit(solution)/shard_map/reduce_scatter | solution.py:112
  56.2 59.8 %reduce-scatter.6.cloned.1.call-start = ((), (), s32[]{:S(2)}) async-start(), calls=%async_computation.7 | async-start | bytes 2752512 | tf_op jit(solution)/shard_map/reduce_scatter | solution.py:115
  58.2 2.0 %copy-start.5 = (u32[32]{0:T(128)S(1)}, u32[32]{0:T(128)}, u32[]{:S(2)}) copy-start(u32[32]{0:T(128)} %constant.34) | copy-start | bytes 388
  58.2 71.2 %reduce-scatter.8.cloned.1.call-start = ((), (), s32[]{:S(2)}) async-start(), calls=%async_computation.8 | async-start | bytes 2752512 | tf_op jit(solution)/shard_map/reduce_scatter | solution.py:119
  92.3 8.4 %all-to-all-start.2 = ((bf16[4,2,3584]{2,1,0:T(2,128)(2,1)}), bf16[4,2,3584]{2,1,0:T(2,128)(2,1)S(1)}, u32[]{:S(2)}, u32[]{:S(2)}) async-start(bf16[4,2,3584]{2,1,0:T(2,128)(2,1)} %copy.43), calls=%async_computation.2 | async-start | bytes 114688 | tf_op jit(solution)/shard_map/all_to_all | solution.py:99
Sparse Core Ops, SparseCore 0:
  9.5 12.9 all-gather.8
  24.1 11.3 all-gather.10
  37.0 11.3 all-gather.6
  54.3 36.3 all-reduce.2
  93.4 9.1 reduce-scatter.3
  105.2 10.6 reduce-scatter.5
  118.8 10.5 reduce-scatter.7
where the time goes:
time: 137 us; the launch traced here: 136 us
  waiting for transfers between devices  68.3 us (50%)
  matrix products  17.8 us (13%)
  between operations  14.9 us (11%)
  blocking collectives  13.7 us (10%)
  starting transfers between devices  12.5 us (9%)
  local copies, waits for them, and re-layouts  8.66 us (6%)
    unnamed x8, waiting for transfers between devices  31.5 us
    all_gather x1, blocking collectives, body(): whole_rows = lax.all_gather(returned, 'tensor', axis=1, tiled=True)  13.7 us
    reduce_scatter x1, waiting for transfers between devices, body(): lax.psum_scatter(term_down.astype(jnp.bfloat16), 'dp', scatter_dimension=...  13.4 us
    all_gather x1, waiting for transfers between devices, body(): down_full = lax.all_gather(down_weight[0], 'dp', axis=1, tiled=True)  11 us
    all_gather x1, waiting for transfers between devices, body(): lax.all_gather(gate_weight[0], 'dp', axis=0, tiled=True)  5.79 us
    all_to_all x1, starting transfers between devices, body(): lax.all_to_all(in_rows, 'expert', split_axis=0, concat_axis=0, tiled=True)  5.19 us
    all_to_all x1, waiting for transfers between devices, body(): lax.all_to_all(row_part, 'expert', split_axis=0, concat_axis=0, tiled=True)  4.8 us
    all_to_all x1, starting transfers between devices, body(): lax.all_to_all(row_part, 'expert', split_axis=0, concat_axis=0, tiled=True)  3.62 us
  transfers between devices with their start and end apart: 10, of which 7 were waited for; matrix products, arithmetic and copies ran while one was open for 15% of the time, Pallas kernels for 0%

commit v1 on v0

v1 whole, which is shorter than its diff:
```python
import jax
import jax.numpy as jnp
from jax import lax
from jax.experimental import pallas as pl
from jax.experimental.pallas import tpu as pltpu
from jax.sharding import PartitionSpec as P

CAP = 8
MESH = pl.DeviceIdType.MESH
F32 = jnp.float32
BF16 = jnp.bfloat16


def dot(a, b, ca, cb):
    return lax.dot_general(a, b, (((ca,), (cb,)), ((), ())), preferred_element_type=F32)


def make_kernel(nd, ne, nz, tokens, width, half, hidden, top, chunks):
    ni = ne // nz
    order = [z + nz * i for z in range(nz) for i in range(ni)]
    place = {k: p for p, k in enumerate(order)}
    lanes = ne * CAP
    rows = ne * nd * CAP
    wide = half // chunks

    def kernel(
        go_hbm, li_hbm, routes_ref, combine_ref, gw_hbm, uw_hbm, dw_hbm,
        out_ref, gg_ref, gu_ref, gd_ref,
        go, li, gw, uw, dw, send, recv, psend, precv, rowg, rsrecv, retsend, agbuf,
        ld_sem, out_sem, d_send, d_recv, p_send, p_recv, r_send, r_recv,
        t_send, t_recv, a_send, a_recv,
        gg_v, gu_v, gd_v, out_v,
    ):
        d = lax.axis_index("dp")
        e = lax.axis_index("expert")
        z = lax.axis_index("tensor")

        loads = [
            pltpu.make_async_copy(li_hbm, li, ld_sem.at[0]),
            pltpu.make_async_copy(go_hbm, go, ld_sem.at[1]),
            pltpu.make_async_copy(gw_hbm.at[0], gw, ld_sem.at[2]),
            pltpu.make_async_copy(uw_hbm.at[0], uw, ld_sem.at[3]),
            pltpu.make_async_copy(dw_hbm.at[0], dw, ld_sem.at[4]),
        ]
        for c in loads:
            c.start()

        barrier = pltpu.get_barrier_semaphore()
        peers = 0
        for j in range(nd):
            for k in range(ne):
                if j == 0 and k == 0:
                    continue
                pl.semaphore_signal(
                    barrier, inc=1,
                    device_id=(lax.rem(d + j, nd), lax.rem(e + k, ne), z),
                    device_id_type=MESH,
                )
                peers += 1
        for r in range(1, nz):
            pl.semaphore_signal(
                barrier, inc=1, device_id=(d, e, lax.rem(z + r, nz)), device_id_type=MESH
            )
            peers += 1

        lane = lax.broadcasted_iota(jnp.int32, (tokens, lanes), 1)
        group = lane // CAP
        slot = lane - group * CAP
        label = jnp.zeros((tokens, lanes), jnp.int32)
        for p, k in enumerate(order):
            label = jnp.where(group == p, lax.rem(e + k, ne), label)
        chosen = jnp.zeros((tokens, lanes), F32)
        scale = jnp.zeros((tokens, lanes), F32)
        for c in range(top):
            hit = routes_ref[:, c : c + 1] == label
            chosen = chosen + jnp.where(hit, 1.0, 0.0)
            scale = scale + jnp.where(hit, combine_ref[:, c : c + 1], 0.0)
        row_id = lax.broadcasted_iota(jnp.int32, (tokens, tokens), 0)
        col_id = lax.broadcasted_iota(jnp.int32, (tokens, tokens), 1)
        lower = jnp.where(col_id < row_id, 1.0, 0.0).astype(BF16)
        before = dot(lower, chosen.astype(BF16), 1, 0)
        keep = jnp.logical_and(chosen > 0.0, before == slot.astype(F32))
        pick_f = jnp.where(keep, 1.0, 0.0)
        pick = pick_f.astype(BF16)
        factor = jnp.sum(jnp.transpose(pick_f * scale), axis=1, keepdims=True)

        loads[0].wait()
        loads[1].wait()
        pl.semaphore_wait(barrier, peers)

        def block_of(k, j):
            return k * nd + j

        sends = []
        for j in range(nd - 1, -1, -1):
            dj = lax.rem(d + j, nd)
            off = pl.multiple_of(dj * half, 128)
            in_pick = dot(pick, li[:, pl.ds(off, half)], 0, 0)
            gr_pick = dot(pick, go[:, pl.ds(off, half)], 0, 0) * factor
            for k in range(ne - 1, -1, -1):
                lo = place[k] * CAP
                tile = jnp.concatenate(
                    [in_pick[lo : lo + CAP], gr_pick[lo : lo + CAP]], axis=0
                ).astype(BF16)
                b = block_of(k, j)
                if j == 0 and k == 0:
                    recv[b] = tile
                    continue
                send[b] = tile
                c = pltpu.make_async_remote_copy(
                    src_ref=send.at[b], dst_ref=recv.at[b],
                    send_sem=d_send.at[b], recv_sem=d_recv.at[b],
                    device_id=(dj, lax.rem(e + k, ne), z), device_id_type=MESH,
                )
                c.start()
                sends.append((b, c))
        for c in loads[2:]:
            c.wait()
        for b, c in sends:
            c.wait_recv()

        x = recv[...].reshape(ne * nd * 2 * CAP, half)

        def take(v, which):
            v = v.reshape(ne * nd, 2, CAP, hidden)[:, which]
            return v.reshape(rows, hidden)

        gate = take(dot(x, gw[...], 1, 0), 0)
        up = take(dot(x, uw[...], 1, 0), 0)
        dhid = take(dot(x, dw[...], 1, 1), 1)
        psend[0] = gate.astype(psend.dtype)
        psend[1] = up.astype(psend.dtype)
        psend[2] = dhid.astype(psend.dtype)
        pcopies = []
        for j in range(1, nd):
            c = pltpu.make_async_remote_copy(
                src_ref=psend, dst_ref=precv.at[j - 1],
                send_sem=p_send.at[j - 1], recv_sem=p_recv.at[j - 1],
                device_id=(lax.rem(d + j, nd), e, z), device_id_type=MESH,
            )
            c.start()
            pcopies.append(c)

        def swap(v, j):
            v = v.reshape(ne, nd, CAP, hidden)
            parts = [v[:, (q + nd - j) % nd] for q in range(nd)]
            return jnp.stack(parts, axis=1).reshape(rows, hidden)

        for j, c in enumerate(pcopies, start=1):
            c.wait_recv()
            gate = gate + swap(precv[j - 1, 0].astype(F32), j)
            up = up + swap(precv[j - 1, 1].astype(F32), j)
            dhid = dhid + swap(precv[j - 1, 2].astype(F32), j)

        sigma = jax.nn.sigmoid(gate)
        silu = gate * sigma
        act = silu * up
        d_up = dhid * silu
        d_gate = dhid * up * sigma * (1.0 + gate * (1.0 - sigma))

        row = dot(d_gate.astype(BF16), gw[...], 1, 1) + dot(d_up.astype(BF16), uw[...], 1, 1)
        row = row.astype(BF16).reshape(ne, nd * CAP, half)
        for p, k in enumerate(order):
            rowg[p // ni, p % ni] = row[k]

        rs = []
        for r in range(1, nz):
            zt = lax.rem(z + r, nz)
            c = pltpu.make_async_remote_copy(
                src_ref=rowg.at[zt], dst_ref=rsrecv.at[r - 1],
                send_sem=r_send.at[r - 1], recv_sem=r_recv.at[r - 1],
                device_id=(d, e, zt), device_id_type=MESH,
            )
            c.start()
            rs.append(c)

        def pad(v, which):
            v = v.reshape(ne * nd, CAP, hidden)
            zero = jnp.zeros_like(v)
            pair = [v, zero] if which == 0 else [zero, v]
            return jnp.concatenate(pair, axis=1).reshape(ne * nd * 2 * CAP, hidden).astype(BF16)

        dg_pad = pad(d_gate, 0)
        du_pad = pad(d_up, 0)
        act_pad = pad(act, 1)
        gg_v[...] = (dot(x, dg_pad, 0, 0) * 0.25).astype(BF16)
        o_gg = pltpu.make_async_copy(gg_v, gg_ref.at[0], out_sem.at[0])
        o_gg.start()

        total = rowg[z].astype(F32)
        for r in range(1, nz):
            rs[r - 1].wait_recv()
            total = total + rsrecv[r - 1].astype(F32)
        total = total.reshape(ni, nd, CAP, half)
        retsend[...] = total.astype(BF16)

        def ret_copy(i, j):
            k = z + nz * i
            return pltpu.make_async_remote_copy(
                src_ref=retsend.at[i, j], dst_ref=agbuf.at[z, i, d],
                send_sem=t_send.at[i, j], recv_sem=t_recv.at[i, d],
                device_id=(lax.rem(d + nd - j, nd), lax.rem(e + ne - k, ne), z),
                device_id_type=MESH,
            )

        def own_copy():
            return pltpu.make_async_copy(retsend.at[0, 0], agbuf.at[z, 0, d], t_recv.at[0, d])

        for i in range(ni):
            for j in range(nd):
                if i == 0 and j == 0:
                    @pl.when(z == 0)
                    def _():
                        own_copy().start()

                    @pl.when(z != 0)
                    def _():
                        ret_copy(0, 0).start()
                else:
                    ret_copy(i, j).start()

        gu_v[...] = (dot(x, du_pad, 0, 0) * 0.25).astype(BF16)
        o_gu = pltpu.make_async_copy(gu_v, gu_ref.at[0], out_sem.at[1])
        o_gu.start()

        for i in range(ni):
            for q in range(nd):
                pltpu.make_async_copy(
                    retsend.at[i, q], agbuf.at[z, i, q], t_recv.at[i, q]
                ).wait()
        ag = []
        for r in range(1, nz):
            c = pltpu.make_async_remote_copy(
                src_ref=agbuf.at[z], dst_ref=agbuf.at[z],
                send_sem=a_send.at[r - 1], recv_sem=a_recv.at[r - 1],
                device_id=(d, e, lax.rem(z + r, nz)), device_id_type=MESH,
            )
            c.start()
            ag.append(c)

        gd_v[...] = (dot(act_pad, x, 0, 0) * 0.25).astype(BF16)
        o_gd = pltpu.make_async_copy(gd_v, gd_ref.at[0], out_sem.at[2])
        o_gd.start()

        for r in range(1, nz):
            zs = lax.rem(z + nz - r, nz)
            pltpu.make_async_copy(agbuf.at[zs], agbuf.at[zs], a_recv.at[r - 1]).wait()

        for q in range(nd):
            got = agbuf[:, :, q].astype(F32).reshape(lanes, half).astype(BF16)
            out_v[:, q * half : (q + 1) * half] = dot(pick, got, 1, 0).astype(BF16)
        o_in = pltpu.make_async_copy(out_v, out_ref, out_sem.at[3])
        o_in.start()

        for b, c in sends:
            c.wait_send()
        for c in pcopies:
            c.wait_send()
        for c in rs:
            c.wait_send()
        for i in range(ni):
            for j in range(nd):
                if i == 0 and j == 0:
                    @pl.when(z != 0)
                    def _():
                        ret_copy(0, 0).wait_send()
                else:
                    ret_copy(i, j).wait_send()
        for c in ag:
            c.wait_send()
        for c in (o_gg, o_gu, o_gd, o_in):
            c.wait()

    return kernel


def body(grad_out, layer_in, routes, combine, gate_weight, up_weight, down_weight):
    nd = lax.axis_size("dp")
    ne = lax.axis_size("expert")
    nz = lax.axis_size("tensor")
    tokens, width = grad_out.shape
    top = routes.shape[1]
    half, hidden = gate_weight.shape[1:]
    ni = ne // nz
    blocks = ne * nd
    kernel = make_kernel(nd, ne, nz, tokens, width, half, hidden, top, 1)
    anyspec = pl.BlockSpec(memory_space=pl.ANY)
    vspec = pl.BlockSpec(memory_space=pltpu.VMEM)
    dma = pltpu.SemaphoreType.DMA
    return tuple(
        pl.pallas_call(
            kernel,
            out_shape=(
                jax.ShapeDtypeStruct((tokens, width), BF16),
                jax.ShapeDtypeStruct(gate_weight.shape, BF16),
                jax.ShapeDtypeStruct(up_weight.shape, BF16),
                jax.ShapeDtypeStruct(down_weight.shape, BF16),
            ),
            in_specs=[anyspec, anyspec, vspec, vspec, anyspec, anyspec, anyspec],
            out_specs=(anyspec,) * 4,
            scratch_shapes=[
                pltpu.VMEM((tokens, width), BF16),
                pltpu.VMEM((tokens, width), BF16),
                pltpu.VMEM((half, hidden), BF16),
                pltpu.VMEM((half, hidden), BF16),
                pltpu.VMEM((hidden, half), BF16),
                pltpu.VMEM((blocks, 2 * CAP, half), BF16),
                pltpu.VMEM((blocks, 2 * CAP, half), BF16),
                pltpu.VMEM((3, blocks * CAP, hidden), BF16),
                pltpu.VMEM((nd - 1, 3, blocks * CAP, hidden), BF16),
                pltpu.VMEM((nz, ni, nd * CAP, half), BF16),
                pltpu.VMEM((nz - 1, ni, nd * CAP, half), BF16),
                pltpu.VMEM((ni, nd, CAP, half), BF16),
                pltpu.VMEM((nz, ni, nd, CAP, half), BF16),
                dma((5,)),
                dma((4,)),
                dma((blocks,)),
                dma((blocks,)),
                dma((nd - 1,)),
                dma((nd - 1,)),
                dma((nz - 1,)),
                dma((nz - 1,)),
                dma((ni, nd)),
                dma((ni, nd)),
                dma((nz - 1,)),
                dma((nz - 1,)),
                pltpu.VMEM((half, hidden), BF16),
                pltpu.VMEM((half, hidden), BF16),
                pltpu.VMEM((hidden, half), BF16),
                pltpu.VMEM((tokens, width), BF16),
            ],
            compiler_params=pltpu.CompilerParams(
                collective_id=0, has_side_effects=True, vmem_limit_bytes=60 * 1024 * 1024
            ),
        )(grad_out, layer_in, routes, combine, gate_weight, up_weight, down_weight)
    )


def solution(mesh):
    return jax.shard_map(
        body,
        mesh=mesh,
        in_specs=(
            P(("dp", "expert"), None),
            P(("dp", "expert"), None),
            P(("dp", "expert"), None),
            P(("dp", "expert"), None),
            P("expert", "dp", "tensor"),
            P("expert", "dp", "tensor"),
            P("expert", "tensor", "dp"),
        ),
        out_specs=(
            P(("dp", "expert"), None),
            P("expert", "dp", "tensor"),
            P("expert", "dp", "tensor"),
            P("expert", "tensor", "dp"),
        ),
        check_vma=False,
    )
```

time: 137 us -> 42.3 us (0.31)
  waiting for transfers between devices: 68.3 us -> 0 us
  Pallas kernels: 0 us -> 33 us
  matrix products: 17.8 us -> 0 us
  between operations: 14.9 us -> 0.66 us
  blocking collectives: 13.7 us -> 0 us
  starting transfers between devices: 12.5 us -> 0 us
    pallas_call x0 -> x1, Pallas kernels: none -> 33 us  [body(): pl.pallas_call(kernel, out_shape=(jax.ShapeDtypeStruct((tokens, width), B...]
    unnamed x8 -> x0, waiting for transfers between devices: 31.5 us -> none
    dot_general x11 -> x0, matrix products: 17.8 us -> none  [the longest x1 2.14 us: expert_backward(): lax.dot_general(grad_rows, down_w, (((1,), (1,)), ((), ())), preferred_el...]
    all_gather x3 -> x0, waiting for transfers between devices: 16.8 us -> none  [the longest x1 11 us: body(): down_full = lax.all_gather(down_weight[0], 'dp', axis=1, tiled=True)]
    all_gather x1 -> x0, blocking collectives: 13.7 us -> none  [body(): whole_rows = lax.all_gather(returned, 'tensor', axis=1, tiled=True)]
    reduce_scatter x3 -> x0, waiting for transfers between devices: 13.6 us -> none  [the longest x1 13.4 us: body(): lax.psum_scatter(term_down.astype(jnp.bfloat16), 'dp', scatter_dimension=...]
    all_to_all x3 -> x0, starting transfers between devices: 12.2 us -> none  [the longest x1 5.19 us: body(): lax.all_to_all(in_rows, 'expert', split_axis=0, concat_axis=0, tiled=True)]
    unnamed x14, local copies, waits for them, and re-layouts: 1.47 us -> 8.34 us
  transfers between devices with their start and end apart: 10 -> 0, of which waited for: 7 -> 0; matrix products, arithmetic and copies ran while one was open for 15% -> 0% of each run, Pallas kernels for 0% -> 0%
where the time goes in v1:
time: 42.3 us; the launch traced here: 42 us
  Pallas kernels  33 us (78%)
  local copies, waits for them, and re-layouts  8.34 us (20%)
  between operations  0.66 us (2%)
    pallas_call x1, Pallas kernels, body(): pl.pallas_call(kernel, out_shape=(jax.ShapeDtypeStruct((tokens, width), B...  33 us
    unnamed x14, local copies, waits for them, and re-layouts  8.34 us

profile of v1, /device:TPU:0, one launch (start us, length us, event | category | flops | bytes accessed | tf_op | source)
XLA Modules:
  0.0 42.0 jit_solution(5202227931984864935)
XLA Ops:
  0.6 0.0 copy-start.3
  0.6 1.4 %copy.11.routes_ref = s32[128,8]{1,0:T(8,128)} copy(s32[128,8]{0,1:T(8,128)} %param.9) | data formatting | bytes 8192 | tf_op args[2]
  2.1 0.0 copy-done.3
  2.1 0.7 %copy.12.combine_ref = f32[128,8]{1,0:T(8,128)} copy(f32[128,8]{0,1:T(8,128)S(1)} %copy-done.3) | data formatting | bytes 8192 | tf_op args[3]
  2.8 33.0 %shard_map.102 = (bf16[128,3584]{1,0:T(8,128)(2,1)}, bf16[1,1792,256]{2,1,0:T(8,128)(2,1)}, bf16[1,1792,256]{2,1,0:T(8,128)(2,1)}, bf16[1,256,1792]{2,1,0:T(8,128)(2,1)}) custom-call(bf16[128,3584]{1,0:T(8,128)(2,1)} %go_hbm.1, bf16[128,3584]{1,0:T(8,128)(2,1)} %li_hbm.1, s32[128,8]{1,0:T(8,128)} %copy.11.routes_ref, f32[128,8]{1,0:T(8,128)} %copy.12.combine_ref, ...), custom_call_target="tpu_custom_call" | custom-call | tf_op jit(solution)/shard_map/pallas_call | solution.py:291
  35.8 0.0 copy-start.2
  35.8 2.2 %copy.17 = bf16[128,3584]{1,0:T(8,128)(2,1)} copy(bf16[128,3584]{1,0:T(8,128)(2,1)} %get-tuple-element.8) | data formatting | bytes 1835008
  38.0 0.0 copy-done.2
  38.0 0.0 copy-start.1
  38.0 0.9 %copy.18 = bf16[1,1792,256]{2,1,0:T(8,128)(2,1)} copy(bf16[1,1792,256]{2,1,0:T(8,128)(2,1)S(1)} %copy-done.2) | data formatting | bytes 1835008
  39.0 0.6 %copy-done.1 = bf16[1,1792,256]{2,1,0:T(8,128)(2,1)S(1)} copy-done((bf16[1,1792,256]{2,1,0:T(8,128)(2,1)S(1)}, bf16[1,1792,256]{2,1,0:T(8,128)(2,1)}, u32[]{:S(2)}) %copy-start.1) | copy-done | bytes 917528
  39.5 0.0 copy-start
  39.5 0.9 %copy.19 = bf16[1,1792,256]{2,1,0:T(8,128)(2,1)} copy(bf16[1,1792,256]{2,1,0:T(8,128)(2,1)S(1)} %copy-done.1) | data formatting | bytes 1835008
  40.5 0.6 %copy-done = bf16[1,256,1792]{2,1,0:T(8,128)(2,1)S(1)} copy-done((bf16[1,256,1792]{2,1,0:T(8,128)(2,1)S(1)}, bf16[1,256,1792]{2,1,0:T(8,128)(2,1)}, u32[]{:S(2)}) %copy-start) | copy-done | bytes 917528
  41.1 0.9 %copy.20 = bf16[1,256,1792]{2,1,0:T(8,128)(2,1)} copy(bf16[1,256,1792]{2,1,0:T(8,128)(2,1)S(1)} %copy-done) | data formatting | bytes 1835008
Async XLA Ops:
  0.6 1.4 %copy-start.3 = (f32[128,8]{0,1:T(8,128)S(1)}, f32[128,8]{0,1:T(8,128)}, u32[]{:S(2)}) copy-start(f32[128,8]{0,1:T(8,128)} %param.10) | copy-start | bytes 12292
  35.8 2.3 %copy-start.2 = (bf16[1,1792,256]{2,1,0:T(8,128)(2,1)S(1)}, bf16[1,1792,256]{2,1,0:T(8,128)(2,1)}, u32[]{:S(2)}) copy-start(bf16[1,1792,256]{2,1,0:T(8,128)(2,1)} %get-tuple-element.9) | copy-start | bytes 2752516
  38.0 1.5 %copy-start.1 = (bf16[1,1792,256]{2,1,0:T(8,128)(2,1)S(1)}, bf16[1,1792,256]{2,1,0:T(8,128)(2,1)}, u32[]{:S(2)}) copy-start(bf16[1,1792,256]{2,1,0:T(8,128)(2,1)} %get-tuple-element.10) | copy-start | bytes 2752516
  39.5 1.5 %copy-start = (bf16[1,256,1792]{2,1,0:T(8,128)(2,1)S(1)}, bf16[1,256,1792]{2,1,0:T(8,128)(2,1)}, u32[]{:S(2)}) copy-start(bf16[1,256,1792]{2,1,0:T(8,128)(2,1)} %get-tuple-element.11) | copy-start | bytes 2752516

commit v2 on v1

v2 whole, which is shorter than its diff:
```python
import jax
import jax.numpy as jnp
from jax import lax
from jax.experimental import pallas as pl
from jax.experimental.pallas import tpu as pltpu
from jax.sharding import PartitionSpec as P

CAP = 8
VMEM = 67043328
MESH = pl.DeviceIdType.MESH
F32 = jnp.float32
BF16 = jnp.bfloat16


def dot(a, b, ca, cb):
    return lax.dot_general(a, b, (((ca,), (cb,)), ((), ())), preferred_element_type=F32)


def make_kernel(nd, ne, nz, tokens, width, half, hidden, top, chunks):
    ni = ne // nz
    order = [z + nz * i for z in range(nz) for i in range(ni)]
    place = {k: p for p, k in enumerate(order)}
    lanes = ne * CAP
    rows = ne * nd * CAP
    wide = half // chunks

    def kernel(
        go_hbm, li_hbm, routes_hbm, combine_hbm, gw_hbm, uw_hbm, dw_hbm,
        out_ref, gg_ref, gu_ref, gd_ref,
        go, li, routes, combine, gw, uw, dw, send, recv, psend, precv, rowg, terms, agbuf,
        ld_sem, d_send, d_recv, p_send, p_recv, r_send, r_recv,
        a_send, a_recv,
    ):
        d = lax.axis_index("dp")
        e = lax.axis_index("expert")
        z = lax.axis_index("tensor")

        loads = [
            pltpu.make_async_copy(li_hbm, li, ld_sem.at[0]),
            pltpu.make_async_copy(go_hbm, go, ld_sem.at[1]),
            pltpu.make_async_copy(gw_hbm.at[0], gw, ld_sem.at[2]),
            pltpu.make_async_copy(uw_hbm.at[0], uw, ld_sem.at[3]),
            pltpu.make_async_copy(dw_hbm.at[0], dw, ld_sem.at[4]),
            pltpu.make_async_copy(routes_hbm, routes, ld_sem.at[5]),
            pltpu.make_async_copy(combine_hbm, combine, ld_sem.at[6]),
        ]
        for i in (5, 6, 0, 1, 2, 3, 4):
            loads[i].start()

        barrier = pltpu.get_barrier_semaphore()
        peers = 0
        for j in range(nd):
            for k in range(ne):
                for r in range(nz):
                    if j == 0 and k == 0 and r == 0:
                        continue
                    pl.semaphore_signal(
                        barrier, inc=1,
                        device_id=(lax.rem(d + j, nd), lax.rem(e + k, ne), lax.rem(z + r, nz)),
                        device_id_type=MESH,
                    )
                    peers += 1

        row = lax.broadcasted_iota(jnp.int32, (lanes, tokens), 0)
        group = row // CAP
        slot = row - group * CAP
        label = jnp.zeros((lanes, tokens), jnp.int32)
        for p, k in enumerate(order):
            label = jnp.where(group == p, lax.rem(e + k, ne), label)
        chosen = jnp.zeros((lanes, tokens), F32)
        scale = jnp.zeros((lanes, tokens), F32)
        loads[5].wait()
        loads[6].wait()
        for c in range(top):
            hit = routes[c : c + 1, :] == label
            chosen = chosen + jnp.where(hit, 1.0, 0.0)
            scale = scale + jnp.where(hit, combine[c : c + 1, :], 0.0)
        row_id = lax.broadcasted_iota(jnp.int32, (tokens, tokens), 0)
        col_id = lax.broadcasted_iota(jnp.int32, (tokens, tokens), 1)
        upper = jnp.where(row_id < col_id, 1.0, 0.0).astype(BF16)
        before = dot(chosen.astype(BF16), upper, 1, 0)
        keep = jnp.logical_and(chosen > 0.0, before == slot.astype(F32))
        pick_f = jnp.where(keep, 1.0, 0.0)
        pick = pick_f.astype(BF16)
        factor = jnp.sum(pick_f * scale, axis=1, keepdims=True)

        loads[0].wait()
        loads[1].wait()
        pl.semaphore_wait(barrier, peers)

        def block_of(k, j):
            return k * nd + j

        sends = []
        for j in range(nd - 1, -1, -1):
            dj = lax.rem(d + j, nd)
            off = pl.multiple_of(dj * half, 128)
            in_pick = dot(pick, li[:, pl.ds(off, half)], 1, 0)
            gr_pick = dot(pick, go[:, pl.ds(off, half)], 1, 0) * factor
            for k in range(ne - 1, -1, -1):
                lo = place[k] * CAP
                tile = jnp.concatenate(
                    [in_pick[lo : lo + CAP], gr_pick[lo : lo + CAP]], axis=0
                ).astype(BF16)
                b = block_of(k, j)
                if j == 0 and k == 0:
                    recv[b] = tile
                    continue
                send[b] = tile
                c = pltpu.make_async_remote_copy(
                    src_ref=send.at[b], dst_ref=recv.at[b],
                    send_sem=d_send.at[b], recv_sem=d_recv.at[b],
                    device_id=(dj, lax.rem(e + k, ne), z), device_id_type=MESH,
                )
                c.start()
                sends.append((b, c))
        for c in loads[2:5]:
            c.wait()
        for b, c in sends:
            c.wait_recv()

        x = recv[...].reshape(ne * nd * 2 * CAP, half)

        def take(v, which):
            v = v.reshape(ne * nd, 2, CAP, hidden)[:, which]
            return v.reshape(rows, hidden)

        gate = take(dot(x, gw[...], 1, 0), 0)
        up = take(dot(x, uw[...], 1, 0), 0)
        dhid = take(dot(x, dw[...], 1, 1), 1)
        psend[0] = gate.astype(psend.dtype)
        psend[1] = up.astype(psend.dtype)
        psend[2] = dhid.astype(psend.dtype)
        pcopies = []
        for j in range(1, nd):
            c = pltpu.make_async_remote_copy(
                src_ref=psend, dst_ref=precv.at[j - 1],
                send_sem=p_send.at[j - 1], recv_sem=p_recv.at[j - 1],
                device_id=(lax.rem(d + j, nd), e, z), device_id_type=MESH,
            )
            c.start()
            pcopies.append(c)

        def swap(v, j):
            v = v.reshape(ne, nd, CAP, hidden)
            parts = [v[:, (q + nd - j) % nd] for q in range(nd)]
            return jnp.stack(parts, axis=1).reshape(rows, hidden)

        for j, c in enumerate(pcopies, start=1):
            c.wait_recv()
            gate = gate + swap(precv[j - 1, 0].astype(F32), j)
            up = up + swap(precv[j - 1, 1].astype(F32), j)
            dhid = dhid + swap(precv[j - 1, 2].astype(F32), j)

        sigma = jax.nn.sigmoid(gate)
        silu = gate * sigma
        act = silu * up
        d_up = dhid * silu
        d_gate = dhid * up * sigma * (1.0 + gate * (1.0 - sigma))

        grad = dot(d_gate.astype(BF16), gw[...], 1, 1) + dot(d_up.astype(BF16), uw[...], 1, 1)
        grad = grad.reshape(ne, nd, CAP, half)
        for k in range(ne):
            for j in range(nd):
                rowg[k, j] = grad[k, j].astype(BF16)

        def term_copy(k, j):
            return pltpu.make_async_remote_copy(
                src_ref=rowg.at[k, j], dst_ref=terms.at[z, k // nz, d],
                send_sem=r_send.at[k, j], recv_sem=r_recv.at[z, k // nz, d],
                device_id=(lax.rem(d + nd - j, nd), lax.rem(e + ne - k, ne), k % nz),
                device_id_type=MESH,
            )

        own = pltpu.make_async_copy(rowg.at[0, 0], terms.at[0, 0, d], r_recv.at[0, 0, d])
        for k in range(ne - 1, -1, -1):
            for j in range(nd):
                if k == 0 and j == 0:
                    @pl.when(z == 0)
                    def _():
                        own.start()

                    @pl.when(z != 0)
                    def _():
                        term_copy(0, 0).start()
                else:
                    term_copy(k, j).start()

        def pad(v, which):
            v = v.reshape(ne * nd, CAP, hidden)
            zero = jnp.zeros_like(v)
            pair = [v, zero] if which == 0 else [zero, v]
            return jnp.concatenate(pair, axis=1).reshape(ne * nd * 2 * CAP, hidden).astype(BF16)

        dg_pad = pad(d_gate, 0)
        du_pad = pad(d_up, 0)
        act_pad = pad(act, 1)
        gg_ref[0] = (dot(x, dg_pad, 0, 0) * 0.25).astype(BF16)
        gu_ref[0] = (dot(x, du_pad, 0, 0) * 0.25).astype(BF16)

        total = jnp.zeros((ni, nd, CAP, half), F32)
        for q in range(nz):
            for i in range(ni):
                for h in range(nd):
                    pltpu.make_async_copy(
                        terms.at[q, i, h], terms.at[q, i, h], r_recv.at[q, i, h]
                    ).wait()
            total = total + terms[q].astype(F32)
        agbuf[z] = total.astype(BF16)
        ag = []
        for r in range(1, nz):
            c = pltpu.make_async_remote_copy(
                src_ref=agbuf.at[z], dst_ref=agbuf.at[z],
                send_sem=a_send.at[r - 1], recv_sem=a_recv.at[r - 1],
                device_id=(d, e, lax.rem(z + r, nz)), device_id_type=MESH,
            )
            c.start()
            ag.append(c)

        gd_ref[0] = (dot(act_pad, x, 0, 0) * 0.25).astype(BF16)
        for r in range(1, nz):
            zs = lax.rem(z + nz - r, nz)
            pltpu.make_async_copy(agbuf.at[zs], agbuf.at[zs], a_recv.at[r - 1]).wait()

        for q in range(nd):
            got = agbuf[:, :, q].astype(F32).reshape(lanes, half).astype(BF16)
            out_ref[:, q * half : (q + 1) * half] = dot(pick, got, 0, 0).astype(BF16)
        for b, c in sends:
            c.wait_send()
        for c in pcopies:
            c.wait_send()
        for k in range(ne):
            for j in range(nd):
                if k == 0 and j == 0:
                    @pl.when(z != 0)
                    def _():
                        term_copy(0, 0).wait_send()
                else:
                    term_copy(k, j).wait_send()
        for c in ag:
            c.wait_send()

    return kernel


def body(grad_out, layer_in, routes, combine, gate_weight, up_weight, down_weight):
    nd = lax.axis_size("dp")
    ne = lax.axis_size("expert")
    nz = lax.axis_size("tensor")
    tokens, width = grad_out.shape
    top = routes.shape[1]
    half, hidden = gate_weight.shape[1:]
    ni = ne // nz
    blocks = ne * nd
    kernel = make_kernel(nd, ne, nz, tokens, width, half, hidden, top, 1)
    hbm = pl.BlockSpec(memory_space=pltpu.HBM)
    vmem = pl.BlockSpec(memory_space=pltpu.VMEM)
    dma = pltpu.SemaphoreType.DMA
    held = 2 * (tokens * width + 3 * half * hidden)
    room = VMEM - held
    parts = pl.pallas_call(
            kernel,
            out_shape=(
                pltpu.VMEM((tokens, width), BF16),
                pltpu.VMEM(gate_weight.shape, BF16),
                pltpu.VMEM(up_weight.shape, BF16),
                pltpu.VMEM(down_weight.shape, BF16),
            ),
            in_specs=[hbm] * 7,
            out_specs=(vmem,) * 4,
            scratch_shapes=[
                pltpu.VMEM((tokens, width), BF16),
                pltpu.VMEM((tokens, width), BF16),
                pltpu.VMEM((top, tokens), jnp.int32),
                pltpu.VMEM((top, tokens), F32),
                pltpu.VMEM((half, hidden), BF16),
                pltpu.VMEM((half, hidden), BF16),
                pltpu.VMEM((hidden, half), BF16),
                pltpu.VMEM((blocks, 2 * CAP, half), BF16),
                pltpu.VMEM((blocks, 2 * CAP, half), BF16),
                pltpu.VMEM((3, blocks * CAP, hidden), BF16),
                pltpu.VMEM((nd - 1, 3, blocks * CAP, hidden), BF16),
                pltpu.VMEM((ne, nd, CAP, half), BF16),
                pltpu.VMEM((nz, ni, nd, CAP, half), BF16),
                pltpu.VMEM((nz, ni, nd, CAP, half), BF16),
                dma((7,)),
                dma((blocks,)),
                dma((blocks,)),
                dma((nd - 1,)),
                dma((nd - 1,)),
                dma((ne, nd)),
                dma((nz, ni, nd)),
                dma((nz - 1,)),
                dma((nz - 1,)),
            ],
            compiler_params=pltpu.CompilerParams(
                collective_id=0, has_side_effects=True, vmem_limit_bytes=room
            ),
        )(grad_out, layer_in, routes.T, combine.T, gate_weight, up_weight, down_weight)
    return tuple(parts)


def solution(mesh):
    return jax.shard_map(
        body,
        mesh=mesh,
        in_specs=(
            P(("dp", "expert"), None),
            P(("dp", "expert"), None),
            P(("dp", "expert"), None),
            P(("dp", "expert"), None),
            P("expert", "dp", "tensor"),
            P("expert", "dp", "tensor"),
            P("expert", "tensor", "dp"),
        ),
        out_specs=(
            P(("dp", "expert"), None),
            P("expert", "dp", "tensor"),
            P("expert", "dp", "tensor"),
            P("expert", "tensor", "dp"),
        ),
        check_vma=False,
    )
```

time: 42.3 us -> 35.1 us (0.83)
  local copies, waits for them, and re-layouts: 8.34 us -> 3.69 us
  Pallas kernels: 33 us -> 30.6 us
    unnamed x14 -> x4, local copies, waits for them, and re-layouts: 8.34 us -> 3.69 us
    pallas_call x1, Pallas kernels: 33 us -> 30.6 us  [body(): pl.pallas_call(kernel, out_shape=(pltpu.VMEM((tokens, width), BF16), pltp...]
where the time goes in v2:
time: 35.1 us; the launch traced here: 35 us
  Pallas kernels  30.6 us (87%)
  local copies, waits for them, and re-layouts  3.69 us (11%)
  between operations  0.64 us (2%)
    pallas_call x1, Pallas kernels, body(): pl.pallas_call(kernel, out_shape=(pltpu.VMEM((tokens, width), BF16), pltp...  30.6 us
    unnamed x4, local copies, waits for them, and re-layouts  3.69 us

profile of v2, /device:TPU:0, one launch (start us, length us, event | category | flops | bytes accessed | tf_op | source)
XLA Modules:
  0.0 35.0 jit_solution(7483944935930242834)
XLA Ops:
  0.6 30.6 %shard_map.102 = (bf16[128,3584]{1,0:T(8,128)(2,1)S(1)}, bf16[1,1792,256]{2,1,0:T(8,128)(2,1)S(1)}, bf16[1,1792,256]{2,1,0:T(8,128)(2,1)S(1)}, bf16[1,256,1792]{2,1,0:T(8,128)(2,1)S(1)}) custom-call(bf16[128,3584]{1,0:T(8,128)(2,1)} %go_hbm.1, bf16[128,3584]{1,0:T(8,128)(2,1)} %li_hbm.1, s32[8,128]{1,0:T(8,128)} %bitcast.2, f32[8,128]{1,0:T(8,128)} %bitcast.3, ...), custom_call_target="tpu_custom_call" | custom-call | tf_op jit(solution)/shard_map/pallas_call | solution.py:261
  31.3 0.9 %copy.15 = bf16[128,3584]{1,0:T(8,128)(2,1)} copy(bf16[128,3584]{1,0:T(8,128)(2,1)S(1)} %get-tuple-element.4) | data formatting | bytes 1835008
  32.2 0.9 %copy.16 = bf16[1,1792,256]{2,1,0:T(8,128)(2,1)} copy(bf16[1,1792,256]{2,1,0:T(8,128)(2,1)S(1)} %get-tuple-element.5) | data formatting | bytes 1835008
  33.1 0.9 %copy.17 = bf16[1,1792,256]{2,1,0:T(8,128)(2,1)} copy(bf16[1,1792,256]{2,1,0:T(8,128)(2,1)S(1)} %get-tuple-element.6) | data formatting | bytes 1835008
  34.0 0.9 %copy.18 = bf16[1,256,1792]{2,1,0:T(8,128)(2,1)} copy(bf16[1,256,1792]{2,1,0:T(8,128)(2,1)S(1)} %get-tuple-element.7) | data formatting | bytes 1835008

commit v3 on v2

--- a/solution.py
+++ b/solution.py
@@ -6,6 +6,8 @@
 from jax.sharding import PartitionSpec as P
 
 CAP = 8
+OUT_PARTS = 2
+BACK_PARTS = 2
 VMEM = 67043328
 MESH = pl.DeviceIdType.MESH
 F32 = jnp.float32
@@ -16,13 +18,20 @@
     return lax.dot_general(a, b, (((ca,), (cb,)), ((), ())), preferred_element_type=F32)
 
 
-def make_kernel(nd, ne, nz, tokens, width, half, hidden, top, chunks):
+def cuts(extent, parts):
+    tiles = extent // 128
+    edges = [128 * ((tiles * c + parts - 1) // parts) for c in range(parts + 1)]
+    return list(zip(edges[:-1], edges[1:]))
+
+
+def make_kernel(nd, ne, nz, tokens, width, half, hidden, top):
     ni = ne // nz
     order = [z + nz * i for z in range(nz) for i in range(ni)]
     place = {k: p for p, k in enumerate(order)}
     lanes = ne * CAP
     rows = ne * nd * CAP
-    wide = half // chunks
+    out_cuts = cuts(half, OUT_PARTS)
+    back_cuts = cuts(half, BACK_PARTS)
 
     def kernel(
         go_hbm, li_hbm, routes_hbm, combine_hbm, gw_hbm, uw_hbm, dw_hbm,
@@ -86,48 +95,55 @@
 
         loads[0].wait()
         loads[1].wait()
-        pl.semaphore_wait(barrier, peers)
-
-        def block_of(k, j):
-            return k * nd + j
 
         sends = []
-        for j in range(nd - 1, -1, -1):
-            dj = lax.rem(d + j, nd)
-            off = pl.multiple_of(dj * half, 128)
-            in_pick = dot(pick, li[:, pl.ds(off, half)], 1, 0)
-            gr_pick = dot(pick, go[:, pl.ds(off, half)], 1, 0) * factor
-            for k in range(ne - 1, -1, -1):
-                lo = place[k] * CAP
-                tile = jnp.concatenate(
-                    [in_pick[lo : lo + CAP], gr_pick[lo : lo + CAP]], axis=0
-                ).astype(BF16)
-                b = block_of(k, j)
-                if j == 0 and k == 0:
-                    recv[b] = tile
-                    continue
-                send[b] = tile
-                c = pltpu.make_async_remote_copy(
-                    src_ref=send.at[b], dst_ref=recv.at[b],
-                    send_sem=d_send.at[b], recv_sem=d_recv.at[b],
-                    device_id=(dj, lax.rem(e + k, ne), z), device_id_type=MESH,
-                )
-                c.start()
-                sends.append((b, c))
+        for c, (lo, hi) in enumerate(out_cuts):
+            for j in range(nd - 1, -1, -1):
+                dj = lax.rem(d + j, nd)
+                span = pl.ds(pl.multiple_of(dj * half + lo, 128), hi - lo)
+                in_pick = dot(pick, li[:, span], 1, 0)
+                gr_pick = dot(pick, go[:, span], 1, 0) * factor
+                if not sends:
+                    pl.semaphore_wait(barrier, peers)
+                for k in range(ne - 1, -1, -1):
+                    at = place[k] * CAP
+                    tile = jnp.concatenate(
+                        [in_pick[at : at + CAP], gr_pick[at : at + CAP]], axis=0
+                    ).astype(BF16)
+                    b = k * nd + j
+                    if j == 0 and k == 0:
+                        recv[b, :, lo:hi] = tile
+                        continue
+                    send[b, :, lo:hi] = tile
+                    copy = pltpu.make_async_remote_copy(
+                        src_ref=send.at[b, :, pl.ds(lo, hi - lo)],
+                        dst_ref=recv.at[b, :, pl.ds(lo, hi - lo)],
+                        send_sem=d_send.at[b, c], recv_sem=d_recv.at[b, c],
+                        device_id=(dj, lax.rem(e + k, ne), z), device_id_type=MESH,
+                    )
+                    copy.start()
+                    sends.append((c, copy))
         for c in loads[2:5]:
             c.wait()
-        for b, c in sends:
-            c.wait_recv()
-
-        x = recv[...].reshape(ne * nd * 2 * CAP, half)
+
+        every = ne * nd * 2 * CAP
+        gate = jnp.zeros((every, hidden), F32)
+        up = jnp.zeros((every, hidden), F32)
+        dhid = jnp.zeros((every, hidden), F32)
+        for c, (lo, hi) in enumerate(out_cuts):
+            for part, copy in sends:
+                if part == c:
+                    copy.wait_recv()
+            xc = recv[:, :, lo:hi].reshape(every, hi - lo)
+            gate = gate + dot(xc, gw[lo:hi, :], 1, 0)
+            up = up + dot(xc, uw[lo:hi, :], 1, 0)
+            dhid = dhid + dot(xc, dw[:, lo:hi], 1, 1)
 
         def take(v, which):
             v = v.reshape(ne * nd, 2, CAP, hidden)[:, which]
             return v.reshape(rows, hidden)
 
-        gate = take(dot(x, gw[...], 1, 0), 0)
-        up = take(dot(x, uw[...], 1, 0), 0)
-        dhid = take(dot(x, dw[...], 1, 1), 1)
+        gate, up, dhid = take(gate, 0), take(up, 0), take(dhid, 1)
         psend[0] = gate.astype(psend.dtype)
         psend[1] = up.astype(psend.dtype)
         psend[2] = dhid.astype(psend.dtype)
@@ -158,33 +174,40 @@
         d_up = dhid * silu
         d_gate = dhid * up * sigma * (1.0 + gate * (1.0 - sigma))
 
-        grad = dot(d_gate.astype(BF16), gw[...], 1, 1) + dot(d_up.astype(BF16), uw[...], 1, 1)
-        grad = grad.reshape(ne, nd, CAP, half)
-        for k in range(ne):
-            for j in range(nd):
-                rowg[k, j] = grad[k, j].astype(BF16)
-
-        def term_copy(k, j):
+        def term_copy(k, j, c):
+            lo, hi = back_cuts[c]
+            span = pl.ds(lo, hi - lo)
             return pltpu.make_async_remote_copy(
-                src_ref=rowg.at[k, j], dst_ref=terms.at[z, k // nz, d],
-                send_sem=r_send.at[k, j], recv_sem=r_recv.at[z, k // nz, d],
+                src_ref=rowg.at[k, j, :, span], dst_ref=terms.at[z, k // nz, d, :, span],
+                send_sem=r_send.at[k, j, c], recv_sem=r_recv.at[z, k // nz, d, c],
                 device_id=(lax.rem(d + nd - j, nd), lax.rem(e + ne - k, ne), k % nz),
                 device_id_type=MESH,
             )
 
-        own = pltpu.make_async_copy(rowg.at[0, 0], terms.at[0, 0, d], r_recv.at[0, 0, d])
-        for k in range(ne - 1, -1, -1):
-            for j in range(nd):
-                if k == 0 and j == 0:
-                    @pl.when(z == 0)
-                    def _():
-                        own.start()
-
-                    @pl.when(z != 0)
-                    def _():
-                        term_copy(0, 0).start()
-                else:
-                    term_copy(k, j).start()
+        def own_copy(c):
+            lo, hi = back_cuts[c]
+            span = pl.ds(lo, hi - lo)
+            return pltpu.make_async_copy(
+                rowg.at[0, 0, :, span], terms.at[0, 0, d, :, span], r_recv.at[0, 0, d, c]
+            )
+
+        dg_bf, du_bf = d_gate.astype(BF16), d_up.astype(BF16)
+        for c, (lo, hi) in enumerate(back_cuts):
+            grad = dot(dg_bf, gw[lo:hi, :], 1, 1) + dot(du_bf, uw[lo:hi, :], 1, 1)
+            grad = grad.reshape(ne, nd, CAP, hi - lo)
+            for k in range(ne - 1, -1, -1):
+                for j in range(nd):
+                    rowg[k, j, :, lo:hi] = grad[k, j].astype(BF16)
+                    if k == 0 and j == 0:
+                        @pl.when(z == 0)
+                        def _():
+                            own_copy(c).start()
+
+                        @pl.when(z != 0)
+                        def _():
+                            term_copy(0, 0, c).start()
+                    else:
+                        term_copy(k, j, c).start()
 
         def pad(v, which):
             v = v.reshape(ne * nd, CAP, hidden)
@@ -195,48 +218,53 @@
         dg_pad = pad(d_gate, 0)
         du_pad = pad(d_up, 0)
         act_pad = pad(act, 1)
+        x = recv[...].reshape(every, half)
         gg_ref[0] = (dot(x, dg_pad, 0, 0) * 0.25).astype(BF16)
         gu_ref[0] = (dot(x, du_pad, 0, 0) * 0.25).astype(BF16)
-
-        total = jnp.zeros((ni, nd, CAP, half), F32)
-        for q in range(nz):
-            for i in range(ni):
-                for h in range(nd):
-                    pltpu.make_async_copy(
-                        terms.at[q, i, h], terms.at[q, i, h], r_recv.at[q, i, h]
-                    ).wait()
-            total = total + terms[q].astype(F32)
-        agbuf[z] = total.astype(BF16)
+        gd_ref[0] = (dot(act_pad, x, 0, 0) * 0.25).astype(BF16)
+
         ag = []
-        for r in range(1, nz):
-            c = pltpu.make_async_remote_copy(
-                src_ref=agbuf.at[z], dst_ref=agbuf.at[z],
-                send_sem=a_send.at[r - 1], recv_sem=a_recv.at[r - 1],
-                device_id=(d, e, lax.rem(z + r, nz)), device_id_type=MESH,
-            )
-            c.start()
-            ag.append(c)
-
-        gd_ref[0] = (dot(act_pad, x, 0, 0) * 0.25).astype(BF16)
-        for r in range(1, nz):
-            zs = lax.rem(z + nz - r, nz)
-            pltpu.make_async_copy(agbuf.at[zs], agbuf.at[zs], a_recv.at[r - 1]).wait()
-
-        for q in range(nd):
-            got = agbuf[:, :, q].astype(F32).reshape(lanes, half).astype(BF16)
-            out_ref[:, q * half : (q + 1) * half] = dot(pick, got, 0, 0).astype(BF16)
-        for b, c in sends:
-            c.wait_send()
+        for c, (lo, hi) in enumerate(back_cuts):
+            span = pl.ds(lo, hi - lo)
+            total = jnp.zeros((ni, nd, CAP, hi - lo), F32)
+            for q in range(nz):
+                for i in range(ni):
+                    for h in range(nd):
+                        ref = terms.at[q, i, h, :, span]
+                        pltpu.make_async_copy(ref, ref, r_recv.at[q, i, h, c]).wait()
+                total = total + terms[q, :, :, :, lo:hi].astype(F32)
+            agbuf[z, :, :, :, lo:hi] = total.astype(BF16)
+            ref = agbuf.at[z, :, :, :, span]
+            for r in range(1, nz):
+                copy = pltpu.make_async_remote_copy(
+                    src_ref=ref, dst_ref=ref,
+                    send_sem=a_send.at[r - 1, c], recv_sem=a_recv.at[r - 1, c],
+                    device_id=(d, e, lax.rem(z + r, nz)), device_id_type=MESH,
+                )
+                copy.start()
+                ag.append(copy)
+
+        for c, (lo, hi) in enumerate(back_cuts):
+            for r in range(1, nz):
+                ref = agbuf.at[lax.rem(z + nz - r, nz), :, :, :, pl.ds(lo, hi - lo)]
+                pltpu.make_async_copy(ref, ref, a_recv.at[r - 1, c]).wait()
+            for q in range(nd):
+                got = agbuf[:, :, q, :, lo:hi].astype(F32).reshape(lanes, hi - lo).astype(BF16)
+                out_ref[:, q * half + lo : q * half + hi] = dot(pick, got, 0, 0).astype(BF16)
+
+        for part, copy in sends:
+            copy.wait_send()
         for c in pcopies:
             c.wait_send()
-        for k in range(ne):
-            for j in range(nd):
-                if k == 0 and j == 0:
-                    @pl.when(z != 0)
-                    def _():
-                        term_copy(0, 0).wait_send()
-                else:
-                    term_copy(k, j).wait_send()
+        for c in range(len(back_cuts)):
+            for k in range(ne):
+                for j in range(nd):
+                    if k == 0 and j == 0:
+                        @pl.when(z != 0)
+                        def _():
+                            term_copy(0, 0, c).wait_send()
+                    else:
+                        term_copy(k, j, c).wait_send()
         for c in ag:
             c.wait_send()
 
@@ -252,7 +280,7 @@
     half, hidden = gate_weight.shape[1:]
     ni = ne // nz
     blocks = ne * nd
-    kernel = make_kernel(nd, ne, nz, tokens, width, half, hidden, top, 1)
+    kernel = make_kernel(nd, ne, nz, tokens, width, half, hidden, top)
     hbm = pl.BlockSpec(memory_space=pltpu.HBM)
     vmem = pl.BlockSpec(memory_space=pltpu.VMEM)
     dma = pltpu.SemaphoreType.DMA
@@ -284,14 +312,14 @@
                 pltpu.VMEM((nz, ni, nd, CAP, half), BF16),
                 pltpu.VMEM((nz, ni, nd, CAP, half), BF16),
                 dma((7,)),
-                dma((blocks,)),
-                dma((blocks,)),
+                dma((blocks, OUT_PARTS)),
+                dma((blocks, OUT_PARTS)),
                 dma((nd - 1,)),
                 dma((nd - 1,)),
-                dma((ne, nd)),
-                dma((nz, ni, nd)),
-                dma((nz - 1,)),
-                dma((nz - 1,)),
+                dma((ne, nd, BACK_PARTS)),
+                dma((nz, ni, nd, BACK_PARTS)),
+                dma((nz - 1, BACK_PARTS)),
+                dma((nz - 1, BACK_PARTS)),
             ],
             compiler_params=pltpu.CompilerParams(
                 collective_id=0, has_side_effects=True, vmem_limit_bytes=room

time: 35.1 us -> 34.2 us (0.974)
  Pallas kernels: 30.6 us -> 29.6 us
    pallas_call x1, Pallas kernels: 30.6 us -> 29.6 us  [body(): pl.pallas_call(kernel, out_shape=(pltpu.VMEM((tokens, width), BF16), pltp...]
where the time goes in v3:
time: 34.2 us; the launch traced here: 34 us
  Pallas kernels  29.6 us (87%)
  local copies, waits for them, and re-layouts  3.69 us (11%)
  between operations  0.64 us (2%)
    pallas_call x1, Pallas kernels, body(): pl.pallas_call(kernel, out_shape=(pltpu.VMEM((tokens, width), BF16), pltp...  29.6 us
    unnamed x4, local copies, waits for them, and re-layouts  3.69 us

profile of v3, /device:TPU:0, one launch (start us, length us, event | category | flops | bytes accessed | tf_op | source)
XLA Modules:
  0.0 34.0 jit_solution(15847416849931874728)
XLA Ops:
  0.6 29.6 %shard_map.102 = (bf16[128,3584]{1,0:T(8,128)(2,1)S(1)}, bf16[1,1792,256]{2,1,0:T(8,128)(2,1)S(1)}, bf16[1,1792,256]{2,1,0:T(8,128)(2,1)S(1)}, bf16[1,256,1792]{2,1,0:T(8,128)(2,1)S(1)}) custom-call(bf16[128,3584]{1,0:T(8,128)(2,1)} %go_hbm.1, bf16[128,3584]{1,0:T(8,128)(2,1)} %li_hbm.1, s32[8,128]{1,0:T(8,128)} %bitcast.2, f32[8,128]{1,0:T(8,128)} %bitcast.3, ...), custom_call_target="tpu_custom_call" | custom-call | tf_op jit(solution)/shard_map/pallas_call | solution.py:289
  30.3 0.9 %copy.15 = bf16[128,3584]{1,0:T(8,128)(2,1)} copy(bf16[128,3584]{1,0:T(8,128)(2,1)S(1)} %get-tuple-element.4) | data formatting | bytes 1835008
  31.2 0.9 %copy.16 = bf16[1,1792,256]{2,1,0:T(8,128)(2,1)} copy(bf16[1,1792,256]{2,1,0:T(8,128)(2,1)S(1)} %get-tuple-element.5) | data formatting | bytes 1835008
  32.1 0.9 %copy.17 = bf16[1,1792,256]{2,1,0:T(8,128)(2,1)} copy(bf16[1,1792,256]{2,1,0:T(8,128)(2,1)S(1)} %get-tuple-element.6) | data formatting | bytes 1835008
  33.1 0.9 %copy.18 = bf16[1,256,1792]{2,1,0:T(8,128)(2,1)} copy(bf16[1,256,1792]{2,1,0:T(8,128)(2,1)S(1)} %get-tuple-element.7) | data formatting | bytes 1835008

commit v4 on v3

--- a/solution.py
+++ b/solution.py
@@ -58,17 +58,21 @@
 
         barrier = pltpu.get_barrier_semaphore()
         peers = 0
-        for j in range(nd):
-            for k in range(ne):
-                for r in range(nz):
-                    if j == 0 and k == 0 and r == 0:
-                        continue
-                    pl.semaphore_signal(
-                        barrier, inc=1,
-                        device_id=(lax.rem(d + j, nd), lax.rem(e + k, ne), lax.rem(z + r, nz)),
-                        device_id_type=MESH,
-                    )
-                    peers += 1
+        for r in range(1, nz):
+            pl.semaphore_signal(
+                barrier, inc=1, device_id=(d, e, lax.rem(z + r, nz)), device_id_type=MESH
+            )
+            peers += 1
+        for k in range(ne - 1, -1, -1):
+            for j in range(nd):
+                if j == 0 and k == 0:
+                    continue
+                pl.semaphore_signal(
+                    barrier, inc=1,
+                    device_id=(lax.rem(d + j, nd), lax.rem(e + k, ne), z),
+                    device_id_type=MESH,
+                )
+                peers += 1
 
         row = lax.broadcasted_iota(jnp.int32, (lanes, tokens), 0)
         group = row // CAP

time: 34.2 us -> 32.7 us (0.956)
  Pallas kernels: 29.6 us -> 28.1 us
    pallas_call x1, Pallas kernels: 29.6 us -> 28.1 us  [body(): pl.pallas_call(kernel, out_shape=(pltpu.VMEM((tokens, width), BF16), pltp...]
where the time goes in v4:
time: 32.7 us; the launch traced here: 32.5 us
  Pallas kernels  28.1 us (86%)
  local copies, waits for them, and re-layouts  3.69 us (11%)
  between operations  0.64 us (2%)
    pallas_call x1, Pallas kernels, body(): pl.pallas_call(kernel, out_shape=(pltpu.VMEM((tokens, width), BF16), pltp...  28.1 us
    unnamed x4, local copies, waits for them, and re-layouts  3.69 us

profile of v4, /device:TPU:0, one launch (start us, length us, event | category | flops | bytes accessed | tf_op | source)
XLA Modules:
  0.0 32.5 jit_solution(15083931227466066594)
XLA Ops:
  0.6 28.1 %shard_map.102 = (bf16[128,3584]{1,0:T(8,128)(2,1)S(1)}, bf16[1,1792,256]{2,1,0:T(8,128)(2,1)S(1)}, bf16[1,1792,256]{2,1,0:T(8,128)(2,1)S(1)}, bf16[1,256,1792]{2,1,0:T(8,128)(2,1)S(1)}) custom-call(bf16[128,3584]{1,0:T(8,128)(2,1)} %go_hbm.1, bf16[128,3584]{1,0:T(8,128)(2,1)} %li_hbm.1, s32[8,128]{1,0:T(8,128)} %bitcast.2, f32[8,128]{1,0:T(8,128)} %bitcast.3, ...), custom_call_target="tpu_custom_call" | custom-call | tf_op jit(solution)/shard_map/pallas_call | solution.py:293
  28.8 0.9 %copy.15 = bf16[128,3584]{1,0:T(8,128)(2,1)} copy(bf16[128,3584]{1,0:T(8,128)(2,1)S(1)} %get-tuple-element.4) | data formatting | bytes 1835008
  29.7 0.9 %copy.16 = bf16[1,1792,256]{2,1,0:T(8,128)(2,1)} copy(bf16[1,1792,256]{2,1,0:T(8,128)(2,1)S(1)} %get-tuple-element.5) | data formatting | bytes 1835008
  30.6 0.9 %copy.17 = bf16[1,1792,256]{2,1,0:T(8,128)(2,1)} copy(bf16[1,1792,256]{2,1,0:T(8,128)(2,1)S(1)} %get-tuple-element.6) | data formatting | bytes 1835008
  31.6 0.9 %copy.18 = bf16[1,256,1792]{2,1,0:T(8,128)(2,1)} copy(bf16[1,256,1792]{2,1,0:T(8,128)(2,1)S(1)} %get-tuple-element.7) | data formatting | bytes 1835008
